TPU v7x, 32 devices: a whole 2x2x4 slice. The times are simulated.
32 devices in a mesh: row: 4 (over z), col: 8 (over y, x, core).
Axes of the slice: x: 2, y: 2, z: 4, core: 2. Of those that a mesh axis runs over, the one named last changes fastest.
Arguments:
- right_side: float32 [16, 1024, 3072], P(None, 'row', 'col'), may hold values from -100 to 100
- cond_x: float32 [1024, 3072], P('row', 'col'), may hold values from 0.25 to 4
- cond_y: float32 [1024, 3072], P('row', 'col'), may hold values from 0.25 to 4
- pad_mask: int32 [1024, 3072], P('row', 'col'), may hold values 0 or 1
Outputs:
- solution: float32 [16, 1024, 3072], P(None, 'row', 'col')
- residual: float32 [16, 1024, 3072], P(None, 'row', 'col')
All inputs are finite; a program needn't handle non-finite values. No bound on the sum of `pad_mask` on one device may be relied on, other than what follows from the above.
Results may differ from a plain program's by a relative error of at most 0.0003.
Values sent between devices are 32-bit elements; how exact they have to be, the bound alone decides.
No kernel may reach another device: no remote copies, remote signals or barrier semaphores. Data moves between devices by JAX's collectives and lax.ppermute only.
A program may use at most 128 MiB of HBM per device.

v0:
```python
import jax
import jax.numpy as jnp
from jax import lax
from jax.sharding import PartitionSpec as P

ITERS = 3


exact_precision = lax.Precision.HIGHEST


def passed_along(shard, axis, by):
    peers = lax.axis_size(axis)
    pairs = [(i, i + by) for i in range(peers) if 0 <= i + by < peers]
    return lax.ppermute(shard, axis, pairs)


def extended(cells, sides, width):
    for axis, dim in sides:
        count = lax.axis_size(axis)
        ends = count - 1
        head = lax.slice_in_dim(cells, 0, width, axis=dim)
        tail = lax.slice_in_dim(cells, cells.shape[dim] - width, cells.shape[dim], axis=dim)
        cells = jnp.concatenate(
            [
                lax.ppermute(tail, axis, [(i, (i + 1) % count) for i in range(ends)]),
                cells,
                lax.ppermute(head, axis, [((i + 1) % count, i) for i in range(ends)]),
            ],
            axis=dim,
        )
    return cells


def neighbour_sum(padded, cond_x, cond_above, cond_y, cond_left):
    total = cond_x * padded[:, 2:, 1:-1] + cond_above * padded[:, :-2, 1:-1]
    return total + cond_y * padded[:, 1:-1, 2:] + cond_left * padded[:, 1:-1, :-2]


def gram(left, right):
    return jnp.einsum("kab,lab->kl", left, right, precision=exact_precision)


def combine(field, matrix):
    return jnp.einsum("kab,kl->lab", field, matrix, precision=exact_precision)


def small_solve(matrix, right):
    factor = jnp.linalg.cholesky(matrix)
    return jax.scipy.linalg.cho_solve((factor, True), right)


def shards(right_side, cond_x, cond_y, pad_mask):
    pad_nodes = pad_mask.astype(jnp.float32)
    free_nodes = 1.0 - pad_nodes
    upper_row = passed_along(cond_x[-1:], "row", 1)
    cond_above = jnp.concatenate([upper_row, cond_x[:-1]], 0)
    left_column = passed_along(cond_y[:, -1:], "col", 1)
    cond_left = jnp.concatenate([left_column, cond_y[:, :-1]], 1)
    diagonal = free_nodes * (cond_x + cond_above + cond_y + cond_left) + pad_nodes
    inverse = 1.0 / diagonal
    solution = jnp.zeros_like(right_side)
    residual = right_side
    precond = residual * inverse
    direction = precond
    gram_now = lax.psum(gram(residual, precond), ("row", "col"))
    for iteration in range(ITERS):
        padded = extended(free_nodes * direction, (("row", 1), ("col", 2)), 1)
        image = pad_nodes * direction + free_nodes * (
            diagonal * direction - neighbour_sum(padded, cond_x, cond_above, cond_y, cond_left)
        )
        weighted = image * inverse
        curvature, cross_term, image_term = lax.psum(
            (gram(direction, image), gram(image, precond), gram(image, weighted)), ("row", "col")
        )
        alpha_block = small_solve(curvature, gram_now)
        solution = solution + combine(direction, alpha_block)
        residual = residual - combine(image, alpha_block)
        precond = residual * inverse
        mixed = jnp.dot(alpha_block.T, cross_term, precision=exact_precision)
        quadratic = jnp.dot(
            jnp.dot(alpha_block.T, image_term, precision=exact_precision),
            alpha_block,
            precision=exact_precision,
        )
        gram_next = gram_now - mixed - mixed.T + quadratic
        beta_block = small_solve(gram_now, gram_next)
        direction = precond + combine(direction, beta_block)
        gram_now = gram_next
    return (solution, residual)


def solution(mesh):
    in_specs = (P(None, "row", "col"), P("row", "col"), P("row", "col"), P("row", "col"))
    out_specs = (P(None, "row", "col"), P(None, "row", "col"))
    return jax.shard_map(shards, mesh=mesh, in_specs=in_specs, out_specs=out_specs, check_vma=False)
```

profile of v0, /device:TPU:0, one launch (start us, length us, event | category | flops | bytes accessed | tf_op | source)
XLA Modules:
  0.0 509.1 jit_solution(3456726133904261827)
XLA Ops:
  1.3 4.9 collective-permute-start
  9.7 2.8 multiply_add_fusion.2
  13.6 6.9 %multiply_multiply_fusion = f32[16,256,384]{2,0,1:T(8,128)S(1)} fusion(f32[16,256,384]{2,1,0:T(8,128)} %param.7, f32[256,384]{1,0:T(8,128)S(1)} %get-tuple-element.31, f32[256,384]{1,0:T(8,128)S(1)} %fusion.83), kind=kLoop, calls=%fused_computation.14 | loop fusion | flops 3145728 | bytes 13369344 | tf_op jit(solution)/shard_map/mul | solution.py:68
  20.5 3.5 collective-permute-start.3
  26.1 3.6 collective-permute-done.2
  29.7 2.7 pad_maximum_fusion.32
  32.4 2.6 copy.30
  35.0 2.6 copy.32
  37.6 3.6 collective-permute-start.5
  42.9 30.7 %fusion.78 = f32[16,16]{0,1:T(8,128)S(1)} fusion(f32[16,256,384]{2,1,0:T(8,128)} %param.7, f32[256,384]{1,0:T(8,128)S(1)} %fusion.83), kind=kOutput, calls=%fused_computation.115 | convolution fusion | flops 303562752 | bytes 6685696 | tf_op jit(solution)/shard_map/kab,lab->kl/dot_general | solution.py:41
  73.6 2.6 copy.31
  76.2 2.5 copy.33
  78.7 21.2 %fusion.14 = f32[16,256,384]{2,0,1:T(8,128)S(1)} fusion(f32[16,258,1]{2,0,1:T(8,128)} %copy.33, f32[16,1,384]{2,0,1:T(8,128)S(1)} %collective-permute-done.2, f32[16,256,384]{2,0,1:T(8,128)} %copy-done.2, f32[16,1,384]{2,0,1:T(8,128)S(1)} %collective-permute-done.3, f32[16,258,1]{2,0,1:T(8,128)} %copy.31, f32[16,256,384]{2,1,0:T(8,128)} %param.7, ...), kind=kLoop, calls=%fused_computation.17 | loop fusion | flops 33030144 | bytes 22102272 | tf_op jit(solution)/shard_map/add | solution.py:69
  99.9 8.1 %fusion.72 = f32[16,16]{1,0:T(8,128)S(1)} fusion(f32[16,256,384]{2,0,1:T(8,128)S(1)} %fusion.14, f32[256,384]{1,0:T(8,128)S(1)} %fusion.83), kind=kOutput, calls=%fused_computation.106 | convolution fusion | flops 303562752 | bytes 6685696 | tf_op jit(solution)/shard_map/kab,lab->kl/dot_general | solution.py:41
  108.1 10.6 %fusion.69 = f32[16,16]{1,0:T(8,128)S(1)} fusion(f32[16,256,384]{2,0,1:T(8,128)S(1)} %fusion.14, f32[16,256,384]{2,1,0:T(8,128)S(1)} %bitcast.144, f32[256,384]{1,0:T(8,128)S(1)} %fusion.83), kind=kOutput, calls=%fused_computation.105 | convolution fusion | flops 303562752 | bytes 12977152 | tf_op jit(solution)/shard_map/kab,lab->kl/dot_general | solution.py:41
  118.7 10.6 %fusion.66 = f32[16,16]{0,1:T(8,128)S(1)} fusion(f32[16,256,384]{2,0,1:T(8,128)S(1)} %fusion.14, f32[16,256,384]{2,1,0:T(8,128)S(1)} %bitcast.144, f32[256,384]{1,0:T(8,128)S(1)} %fusion.83), kind=kOutput, calls=%fused_computation.104 | convolution fusion | flops 303562752 | bytes 12977152 | tf_op jit(solution)/shard_map/kab,lab->kl/dot_general | solution.py:41
  129.2 45.8 %all-reduce.1 = (f32[16,16]{0,1:T(8,128)S(1)}, f32[16,16]{0,1:T(8,128)S(1)}, f32[16,16]{1,0:T(8,128)S(1)}, f32[16,16]{1,0:T(8,128)S(1)}) all-reduce(f32[16,16]{0,1:T(8,128)S(1)} %fusion.78, f32[16,16]{0,1:T(8,128)S(1)} %fusion.66, f32[16,16]{1,0:T(8,128)S(1)} %fusion.72, ...), channel_id=1, replica_groups=mesh['row'=4,'col'=8] {'row','col'}, use_global_device_ids=true, to_apply=%region_3.5 | all-reduce | flops 1024 | bytes 8192 | tf_op jit(solution)/shard_map/psum | solution.py:66
  183.6 13.2 %copy_subtract_fusion = f32[16,256,384]{2,0,1:T(8,128)} fusion(f32[16,256,384]{2,1,0:T(8,128)} %param.7, f32[16,256,384]{2,0,1:T(8,128)} %copy-done, f32[16,16]{1,0:T(8,128)S(1)} %fusion.111), kind=kOutput, calls=%fused_computation.80 | convolution fusion | flops 303562752 | bytes 18875392 | tf_op jit(solution)/shard_map/kab,kl->lab/dot_general | solution.py:45
  199.5 15.0 %broadcast_multiply_fusion.1 = (f32[16,256,384]{2,0,1:T(8,128)S(1)}, f32[16,256,384]{2,0,1:T(8,128)}) fusion(f32[256,384]{1,0:T(8,128)S(1)} %get-tuple-element.31, f32[16,16,1]{0,1,2:T(8,128)S(1)} %convolution_bitcast_fusion.4, f32[16,256,384]{2,1,0:T(8,128)} %param.7, f32[256,384]{1,0:T(8,128)S(1)} %fusion.83, f32[16,256,384]{2,0,1:T(8,128)} %copy_subtract_fusion), kind=kOutput, calls=%fused_computation.83 | convolution fusion | flops 308281344 | bytes 25953280 | tf_op jit(solution)/shard_map/kab,kl->lab/dot_general | solution.py:45
  218.9 3.7 collective-permute-done.6
  222.6 2.7 pad_maximum_fusion.29
  225.3 2.6 copy.43
  227.9 2.6 copy.45
  237.4 2.6 copy.44
  240.0 2.6 copy.46
  242.5 20.3 %fusion.31 = f32[16,256,384]{2,0,1:T(8,128)S(1)} fusion(f32[16,258,1]{2,0,1:T(8,128)} %copy.46, f32[16,1,384]{2,0,1:T(8,128)S(1)} %collective-permute-done.6, f32[16,256,384]{2,0,1:T(8,128)} %copy-done.4, f32[16,1,384]{2,0,1:T(8,128)S(1)} %collective-permute-done.7, f32[16,258,1]{2,0,1:T(8,128)} %copy.44, f32[16,256,384]{2,0,1:T(8,128)} %get-tuple-element.33, ...), kind=kLoop, calls=%fused_computation.43 | loop fusion | flops 31457280 | bytes 21709056 | tf_op jit(solution)/shard_map/add | solution.py:69
  262.9 8.1 %fusion.75 = f32[16,16]{1,0:T(8,128)S(1)} fusion(f32[16,256,384]{2,0,1:T(8,128)S(1)} %fusion.31, f32[256,384]{1,0:T(8,128)S(1)} %fusion.83), kind=kOutput, calls=%fused_computation.107 | convolution fusion | flops 303562752 | bytes 6685696 | tf_op jit(solution)/shard_map/kab,lab->kl/dot_general | solution.py:41
  271.1 8.3 %fusion.63 = f32[16,16]{1,0:T(8,128)S(1)} fusion(f32[16,256,384]{2,0,1:T(8,128)S(1)} %fusion.31, f32[16,256,384]{2,0,1:T(8,128)S(1)} %bitcast.150, f32[256,384]{1,0:T(8,128)S(1)} %fusion.83), kind=kOutput, calls=%fused_computation.103 | convolution fusion | flops 303562752 | bytes 12977152 | tf_op jit(solution)/shard_map/kab,lab->kl/dot_general | solution.py:41
  279.5 8.5 %convolution_bitcast_fusion.3 = f32[16,16]{0,1:T(8,128)S(1)} fusion(f32[16,256,384]{2,0,1:T(8,128)S(1)} %bitcast.148, f32[16,256,384]{2,0,1:T(8,128)S(1)} %fusion.31), kind=kOutput, calls=%fused_computation.112 | convolution fusion | flops 301989888 | bytes 12583936 | tf_op jit(solution)/shard_map/kab,lab->kl/dot_general | solution.py:41
  287.9 41.7 %all-reduce = (f32[16,16]{0,1:T(8,128)S(1)}, f32[16,16]{1,0:T(8,128)S(1)}, f32[16,16]{1,0:T(8,128)S(1)}) all-reduce(f32[16,16]{0,1:T(8,128)S(1)} %convolution_bitcast_fusion.3, f32[16,16]{1,0:T(8,128)S(1)} %fusion.75, f32[16,16]{1,0:T(8,128)S(1)} %fusion.63), channel_id=1, replica_groups=mesh['row'=4,'col'=8] {'row','col'}, use_global_device_ids=true, to_apply=%region_6.0 | all-reduce | flops 768 | bytes 6144 | tf_op jit(solution)/shard_map/psum | solution.py:73
  334.1 10.7 %convolution_subtract_fusion.1 = f32[16,256,384]{2,0,1:T(8,128)} fusion(f32[16,256,384]{2,0,1:T(8,128)} %copy_subtract_fusion, f32[16,256,384]{2,0,1:T(8,128)} %copy-done.1, f32[16,16]{1,0:T(8,128)S(1)} %fusion.100), kind=kOutput, calls=%fused_computation.93 | convolution fusion | flops 303562752 | bytes 18875392 | tf_op jit(solution)/shard_map/kab,kl->lab/dot_general | solution.py:45
  345.9 11.0 %broadcast_multiply_fusion = (f32[16,256,384]{2,0,1:T(8,128)S(1)}, f32[16,256,384]{2,0,1:T(8,128)}) fusion(f32[256,384]{1,0:T(8,128)S(1)} %get-tuple-element.31, f32[16,16,1]{0,1,2:T(8,128)S(1)} %convolution_bitcast_fusion.2, f32[16,256,384]{2,0,1:T(8,128)} %get-tuple-element.33, f32[16,256,384]{2,0,1:T(8,128)} %convolution_subtract_fusion.1, ...), kind=kOutput, calls=%fused_computation.82 | convolution fusion | flops 306708480 | bytes 25953280 | tf_op jit(solution)/shard_map/kab,kl->lab/dot_general | solution.py:45
  356.9 3.1 collective-permute-start.11
  361.5 4.2 collective-permute-done.10
  365.7 2.7 pad_maximum_fusion.26
  368.4 2.6 copy.54
  371.0 2.6 copy.56
  376.3 9.2 %fusion.98 = f32[16,256,384]{2,0,1:T(8,128)} fusion(f32[16,256,384]{2,0,1:T(8,128)} %get-tuple-element.33, f32[16,16]{1,0:T(8,128)S(1)} %fusion.100), kind=kOutput, calls=%fused_computation.144 | convolution fusion | flops 301989888 | bytes 12583936 | tf_op jit(solution)/shard_map/kab,kl->lab/dot_general | solution.py:45
  385.5 2.5 copy.55
  390.6 19.7 %fusion.21 = f32[16,256,384]{2,0,1:T(8,128)S(1)} fusion(f32[16,258,1]{2,0,1:T(8,128)} %copy.57, f32[16,1,384]{2,0,1:T(8,128)S(1)} %collective-permute-done.10, f32[16,256,384]{2,0,1:T(8,128)} %copy-done.3, f32[16,1,384]{2,0,1:T(8,128)S(1)} %collective-permute-done.11, f32[16,258,1]{2,0,1:T(8,128)} %copy.55, f32[16,256,384]{2,0,1:T(8,128)} %get-tuple-element.35, ...), kind=kLoop, calls=%fused_computation.25 | loop fusion | flops 31457280 | bytes 21709056 | tf_op jit(solution)/shard_map/add | solution.py:69
  410.3 2.7 copy-done.5
  413.0 10.2 %convolution_bitcast_fusion.1 = f32[16,16]{0,1:T(8,128)S(1)} fusion(f32[16,256,384]{2,0,1:T(8,128)} %get-tuple-element.35, f32[16,256,384]{2,0,1:T(8,128)S(1)} %fusion.21), kind=kOutput, calls=%fused_computation.109 | convolution fusion | flops 301989888 | bytes 12583936 | tf_op jit(solution)/shard_map/kab,lab->kl/dot_general | solution.py:41
  423.2 43.2 %psum.63 = f32[16,16]{0,1:T(8,128)S(1)} all-reduce(f32[16,16]{0,1:T(8,128)S(1)} %convolution_bitcast_fusion.1), channel_id=1, replica_groups=mesh['row'=4,'col'=8] {'row','col'}, use_global_device_ids=true, to_apply=%region_9.12 | all-reduce | flops 256 | bytes 2048 | tf_op jit(solution)/shard_map/psum | solution.py:73
  470.9 8.9 %convolution_subtract_fusion = f32[16,256,384]{2,0,1:T(8,128)S(1)} fusion(f32[16,256,384]{2,0,1:T(8,128)} %convolution_subtract_fusion.1, f32[16,16,1]{0,1,2:T(8,128)S(1)} %convolution_bitcast_fusion, f32[16,256,384]{2,0,1:T(8,128)} %copy-done.5), kind=kOutput, calls=%fused_computation.92 | convolution fusion | flops 303562752 | bytes 18875392 | tf_op jit(solution)/shard_map/kab,kl->lab/dot_general | solution.py:45
  479.9 7.6 %fusion.123 = f32[16,256,384]{2,0,1:T(8,128)S(1)} fusion(f32[16,16,1]{0,1,2:T(8,128)S(1)} %convolution_bitcast_fusion, f32[16,256,384]{2,0,1:T(8,128)} %get-tuple-element.35), kind=kOutput, calls=%fused_computation.185 | convolution fusion | flops 301989888 | bytes 12583936 | tf_op jit(solution)/shard_map/kab,kl->lab/dot_general | solution.py:45
  487.5 12.1 %add_add_fusion = f32[16,256,384]{2,0,1:T(8,128)S(1)} fusion(f32[16,256,384]{2,0,1:T(8,128)S(1)} %fusion.123, f32[16,256,384]{2,0,1:T(8,128)} %fusion.98, f32[16,256,384]{2,1,0:T(8,128)S(1)} %bitcast.146, f32[256,384]{1,0:T(8,128)S(1)} %fusion.83, f32[16,16]{1,0:T(8,128)S(1)} %fusion.111), kind=kOutput, calls=%fused_computation.72 | convolution fusion | flops 306708480 | bytes 25560064 | tf_op jit(solution)/shard_map/kab,kl->lab/dot_general | solution.py:45
  499.6 4.6 copy.62
  504.3 4.6 copy.63
  (126 shorter events, 48.3 us)
Async XLA Ops:
  1.3 8.4 %collective-permute-start = (f32[1,384]{1,0:T(1,128)S(1)}, f32[1,384]{1,0:T(1,128)S(1)}, u32[]{:S(2)}, u32[]{:S(2)}) collective-permute-start(f32[1,384]{1,0:T(1,128)S(1)} %slice.108), channel_id=1, source_target_pairs={{0,8},{8,16},{16,24},{1,9},{9,17},{17,25},{2,10},{10,18},{18,26},{... | collective-permute-start | bytes 4616 | tf_op jit(solution)/shard_map/ppermute | solution.py:15
  7.3 2.4 collective-permute-start.1
  13.6 11.7 %copy-start.12 = (s32[256,384]{1,0:T(8,128)S(1)}, s32[256,384]{1,0:T(8,128)}, u32[]{:S(2)}) copy-start(s32[256,384]{1,0:T(8,128)} %param.10) | copy-start | bytes 1179652
  20.5 9.2 %copy-start.2 = (f32[16,256,384]{2,0,1:T(8,128)}, f32[16,256,384]{2,0,1:T(8,128)S(1)}, u32[]{:S(2)}) copy-start(f32[16,256,384]{2,0,1:T(8,128)S(1)} %multiply_multiply_fusion) | copy-start | bytes 18874372
  20.5 5.6 %collective-permute-start.3 = (f32[16,1,384]{2,0,1:T(8,128)S(1)}, f32[16,1,384]{2,0,1:T(8,128)S(1)}, u32[]{:S(2)}, u32[]{:S(2)}) collective-permute-start(f32[16,1,384]{2,0,1:T(8,128)S(1)} %get-tuple-element.29), channel_id=1, source_target_pairs={{0,8},{8,16},{16,24},{1,9},{9,17},{17,25},{2,10},{10,18},{18,26},{... | collective-permute-start | bytes 73736 | tf_op jit(solution)/shard_map/ppermute | solution.py:26
  24.0 5.7 %collective-permute-start.2 = (f32[16,1,384]{2,0,1:T(8,128)S(1)}, f32[16,1,384]{2,0,1:T(8,128)S(1)}, u32[]{:S(2)}, u32[]{:S(2)}) collective-permute-start(f32[16,1,384]{2,0,1:T(8,128)S(1)} %get-tuple-element.30), channel_id=1, source_target_pairs={{8,0},{16,8},{24,16},{9,1},{17,9},{25,17},{10,2},{18,10},{26,18},{... | collective-permute-start | bytes 73736 | tf_op jit(solution)/shard_map/ppermute | solution.py:28
  37.6 41.1 %copy-start.6 = (f32[256,384]{1,0:T(8,128)S(1)}, f32[256,384]{1,0:T(8,128)}, u32[]{:S(2)}) copy-start(f32[256,384]{1,0:T(8,128)} %param.9) | copy-start | bytes 1179652
  37.6 38.6 %collective-permute-start.5 = (f32[16,258,1]{1,0,2:T(8,128)S(1)}, f32[16,258,1]{1,0,2:T(8,128)S(1)}, u32[]{:S(2)}, u32[]{:S(2)}) collective-permute-start(f32[16,258,1]{1,0,2:T(8,128)S(1)} %copy.32), channel_id=1, source_target_pairs={{0,1},{1,2},{2,3},{3,4},{4,5},{5,6},{6,7},{8,9},{9,10},{10,11},{11... | collective-permute-start | bytes 49544 | tf_op jit(solution)/shard_map/ppermute | solution.py:26
  41.3 32.4 %collective-permute-start.4 = (f32[16,258,1]{1,0,2:T(8,128)S(1)}, f32[16,258,1]{1,0,2:T(8,128)S(1)}, u32[]{:S(2)}, u32[]{:S(2)}) collective-permute-start(f32[16,258,1]{1,0,2:T(8,128)S(1)} %copy.30), channel_id=1, source_target_pairs={{1,0},{2,1},{3,2},{4,3},{5,4},{6,5},{7,6},{9,8},{10,9},{11,10},{12... | collective-permute-start | bytes 49544 | tf_op jit(solution)/shard_map/ppermute | solution.py:28
  76.2 31.8 %slice-start = ((s8[6291456]{0:T(1024)(128)(4,1)}), s8[2097152]{0:T(1024)(128)(4,1)S(1)}, s32[]{:S(2)}) async-start(s8[6291456]{0:T(1024)(128)(4,1)} %bitcast.143), calls=%async_computation | async-start | bytes 4194304
  78.7 29.3 %slice-start.1 = ((s8[6291456]{0:T(1024)(128)(4,1)}), s8[4194304]{0:T(1024)(128)(4,1)S(1)}, s32[]{:S(2)}) async-start(s8[6291456]{0:T(1024)(128)(4,1)} %bitcast.143), calls=%async_computation.1 | async-start | bytes 8388608
  99.9 18.8 %copy-start = (f32[16,256,384]{2,0,1:T(8,128)}, f32[16,256,384]{2,0,1:T(8,128)S(1)}, u32[]{:S(2)}) copy-start(f32[16,256,384]{2,0,1:T(8,128)S(1)} %fusion.14) | copy-start | bytes 18874372
  214.5 8.1 %copy-start.4 = (f32[16,256,384]{2,0,1:T(8,128)}, f32[16,256,384]{2,0,1:T(8,128)S(1)}, u32[]{:S(2)}) copy-start(f32[16,256,384]{2,0,1:T(8,128)S(1)} %get-tuple-element.32) | copy-start | bytes 18874372
  214.5 4.3 collective-permute-start.7
  216.9 5.7 %collective-permute-start.6 = (f32[16,1,384]{2,0,1:T(8,128)S(1)}, f32[16,1,384]{2,0,1:T(8,128)S(1)}, u32[]{:S(2)}, u32[]{:S(2)}) collective-permute-start(f32[16,1,384]{2,0,1:T(8,128)S(1)} %get-tuple-element.28), channel_id=1, source_target_pairs={{8,0},{16,8},{24,16},{9,1},{17,9},{25,17},{10,2},{18,10},{26,18},{... | collective-permute-start | bytes 73736 | tf_op jit(solution)/shard_map/ppermute | solution.py:28
  230.5 9.5 %collective-permute-start.9 = (f32[16,258,1]{1,0,2:T(8,128)S(1)}, f32[16,258,1]{1,0,2:T(8,128)S(1)}, u32[]{:S(2)}, u32[]{:S(2)}) collective-permute-start(f32[16,258,1]{1,0,2:T(8,128)S(1)} %copy.45), channel_id=1, source_target_pairs={{0,1},{1,2},{2,3},{3,4},{4,5},{5,6},{6,7},{8,9},{9,10},{10,11},{11... | collective-permute-start | bytes 49544 | tf_op jit(solution)/shard_map/ppermute | solution.py:26
  231.8 5.6 %collective-permute-start.8 = (f32[16,258,1]{1,0,2:T(8,128)S(1)}, f32[16,258,1]{1,0,2:T(8,128)S(1)}, u32[]{:S(2)}, u32[]{:S(2)}) collective-permute-start(f32[16,258,1]{1,0,2:T(8,128)S(1)} %copy.43), channel_id=1, source_target_pairs={{1,0},{2,1},{3,2},{4,3},{5,4},{6,5},{7,6},{9,8},{10,9},{11,10},{12... | collective-permute-start | bytes 49544 | tf_op jit(solution)/shard_map/ppermute | solution.py:28
  240.0 31.1 %slice-start.6 = ((s8[6291456]{0:T(1024)(128)(4,1)}), s8[2097152]{0:T(1024)(128)(4,1)S(1)}, s32[]{:S(2)}) async-start(s8[6291456]{0:T(1024)(128)(4,1)} %bitcast.149), calls=%async_computation.6 | async-start | bytes 4194304
  242.5 28.5 %slice-start.7 = ((s8[6291456]{0:T(1024)(128)(4,1)}), s8[4194304]{0:T(1024)(128)(4,1)S(1)}, s32[]{:S(2)}) async-start(s8[6291456]{0:T(1024)(128)(4,1)} %bitcast.149), calls=%async_computation.7 | async-start | bytes 8388608
  262.9 16.6 %copy-start.1 = (f32[16,256,384]{2,0,1:T(8,128)}, f32[16,256,384]{2,0,1:T(8,128)S(1)}, u32[]{:S(2)}) copy-start(f32[16,256,384]{2,0,1:T(8,128)S(1)} %fusion.31) | copy-start | bytes 18874372
  262.9 16.6 %slice-start.4 = ((s8[6291456]{0:T(1024)(128)(4,1)}), s8[4194304]{0:T(1024)(128)(4,1)S(1)}, s32[]{:S(2)}) async-start(s8[6291456]{0:T(1024)(128)(4,1)} %bitcast.147), calls=%async_computation.4 | async-start | bytes 8388608
  271.1 8.4 %slice-start.5 = ((s8[6291456]{0:T(1024)(128)(4,1)}), s8[2097152]{0:T(1024)(128)(4,1)S(1)}, s32[]{:S(2)}) async-start(s8[6291456]{0:T(1024)(128)(4,1)} %bitcast.147), calls=%async_computation.5 | async-start | bytes 4194304
  356.8 8.8 %copy-start.3 = (f32[16,256,384]{2,0,1:T(8,128)}, f32[16,256,384]{2,0,1:T(8,128)S(1)}, u32[]{:S(2)}) copy-start(f32[16,256,384]{2,0,1:T(8,128)S(1)} %get-tuple-element.34) | copy-start | bytes 18874372
  356.9 4.6 collective-permute-start.11
  359.9 5.7 %collective-permute-start.10 = (f32[16,1,384]{2,0,1:T(8,128)S(1)}, f32[16,1,384]{2,0,1:T(8,128)S(1)}, u32[]{:S(2)}, u32[]{:S(2)}) collective-permute-start(f32[16,1,384]{2,0,1:T(8,128)S(1)} %get-tuple-element.26), channel_id=1, source_target_pairs={{8,0},{16,8},{24,16},{9,1},{17,9},{25,17},{10,2},{18,10},{26,18},{... | collective-permute-start | bytes 73736 | tf_op jit(solution)/shard_map/ppermute | solution.py:28
  373.6 17.0 %copy-start.7 = (f32[256,384]{1,0:T(8,128)S(1)}, f32[256,384]{1,0:T(8,128)}, u32[]{:S(2)}) copy-start(f32[256,384]{1,0:T(8,128)} %param.8) | copy-start | bytes 1179652
  373.6 17.0 %copy-start.8 = (f32[256,384]{1,0:T(8,128)S(1)}, f32[256,384]{1,0:T(8,128)}, u32[]{:S(2)}) copy-start(f32[256,384]{1,0:T(8,128)} %get-tuple-element.15) | copy-start | bytes 1179652
  373.6 17.0 %copy-start.9 = (f32[256,384]{1,0:T(8,128)S(1)}, f32[256,384]{1,0:T(8,128)}, u32[]{:S(2)}) copy-start(f32[256,384]{1,0:T(8,128)} %get-tuple-element.17) | copy-start | bytes 1179652
  373.6 17.0 %copy-start.10 = (f32[256,384]{1,0:T(8,128)S(1)}, f32[256,384]{1,0:T(8,128)}, u32[]{:S(2)}) copy-start(f32[256,384]{1,0:T(8,128)} %get-tuple-element.18) | copy-start | bytes 1179652
  373.6 17.0 %copy-start.11 = (f32[256,384]{1,0:T(8,128)S(1)}, f32[256,384]{1,0:T(8,128)}, u32[]{:S(2)}) copy-start(f32[256,384]{1,0:T(8,128)} %convert_element_type.3) | copy-start | bytes 1179652
  373.6 14.4 %collective-permute-start.13 = (f32[16,258,1]{1,0,2:T(8,128)S(1)}, f32[16,258,1]{1,0,2:T(8,128)S(1)}, u32[]{:S(2)}, u32[]{:S(2)}) collective-permute-start(f32[16,258,1]{1,0,2:T(8,128)S(1)} %copy.56), channel_id=1, source_target_pairs={{0,1},{1,2},{2,3},{3,4},{4,5},{5,6},{6,7},{8,9},{9,10},{10,11},{11... | collective-permute-start | bytes 49544 | tf_op jit(solution)/shard_map/ppermute | solution.py:26
  375.0 10.5 %collective-permute-start.12 = (f32[16,258,1]{1,0,2:T(8,128)S(1)}, f32[16,258,1]{1,0,2:T(8,128)S(1)}, u32[]{:S(2)}, u32[]{:S(2)}) collective-permute-start(f32[16,258,1]{1,0,2:T(8,128)S(1)} %copy.54), channel_id=1, source_target_pairs={{1,0},{2,1},{3,2},{4,3},{5,4},{6,5},{7,6},{9,8},{10,9},{11,10},{12... | collective-permute-start | bytes 49544 | tf_op jit(solution)/shard_map/ppermute | solution.py:28
  410.3 2.7 copy-start.5
  413.0 74.5 %slice-start.2 = ((s8[6291456]{0:T(1024)(128)(4,1)}), s8[2097152]{0:T(1024)(128)(4,1)S(1)}, s32[]{:S(2)}) async-start(s8[6291456]{0:T(1024)(128)(4,1)} %bitcast.145), calls=%async_computation.2 | async-start | bytes 4194304
  470.9 16.6 %slice-start.3 = ((s8[6291456]{0:T(1024)(128)(4,1)}), s8[4194304]{0:T(1024)(128)(4,1)S(1)}, s32[]{:S(2)}) async-start(s8[6291456]{0:T(1024)(128)(4,1)} %bitcast.145), calls=%async_computation.3 | async-start | bytes 8388608
where the time goes:
time: 516 us; the launch traced here: 509 us
  matrix products  186 us (36%)
  blocking collectives  131 us (25%)
  other arithmetic  101 us (20%)
  local copies, waits for them, and re-layouts  45.3 us (9%)
  starting transfers between devices  30 us (6%)
  waiting for transfers between devices  15 us (3%)
    dot_general x8, matrix products, gram(): return jnp.einsum('kab,lab->kl', left, right, precision=exact_precision)  95.2 us
    dot_general x8, matrix products, combine(): return jnp.einsum('kab,kl->lab', field, matrix, precision=exact_precision)  87.7 us
    psum x2, blocking collectives, shards(): lax.psum((gram(direction, image), gram(image, precond), gram(image, weigh...  84.9 us
    add x3, other arithmetic, shards(): pad_nodes * direction  61.2 us
    psum x1, blocking collectives, shards(): gram_now = lax.psum(gram(residual, precond), ('row', 'col'))  45.8 us
    ppermute x6, starting transfers between devices, extended(): lax.ppermute(tail, axis, [(i, (i + 1) % count) for i in range(ends)])  15.2 us
    ppermute x6, waiting for transfers between devices, extended(): lax.ppermute(head, axis, [((i + 1) % count, i) for i in range(ends)])  14 us
    unnamed x44, local copies, waits for them, and re-layouts  12.1 us
  transfers between devices with their start and end apart: 14, of which 5 were waited for; matrix products, arithmetic and copies ran while one was open for 10% of the time, Pallas kernels for 0%

commit v1 on v0

v1 whole, which is shorter than its diff:
```python
import functools

import jax
import jax.numpy as jnp
from jax import lax
from jax.experimental import pallas as pl
from jax.experimental.pallas import tpu as pltpu
from jax.sharding import PartitionSpec as P

ITERS = 3
DEPTH = ITERS + 1
SUB = 8
LANE = 128
MOMENTS = 2 * ITERS

exact = lax.Precision.HIGHEST


def split(x):
    high = x.astype(jnp.bfloat16)
    low = (x - high.astype(jnp.float32)).astype(jnp.bfloat16)
    return high, low


def rows_of(ref, k, start):
    return ref[k, pl.ds(pl.multiple_of(start, SUB), SUB), :]


def plane_rows(ref, start):
    return ref[pl.ds(pl.multiple_of(start, SUB), SUB), :]


def stencil(ref, k, slab, last, coefs, row):
    above = rows_of(ref, k, jnp.maximum(slab - 1, 0) * SUB)
    here = rows_of(ref, k, slab * SUB)
    below = rows_of(ref, k, jnp.minimum(slab + 1, last) * SUB)
    down = pltpu.roll(jnp.where(row == 0, below, here), SUB - 1, 0)
    up = pltpu.roll(jnp.where(row == SUB - 1, above, here), 1, 0)
    wide = here.shape[1]
    right = pltpu.roll(here, wide - 1, 1)
    left = pltpu.roll(here, 1, 1)
    to_down, to_up, to_right, to_left = coefs
    return here, (to_down * down + to_up * up) + (to_right * right + to_left * left)


def nt_dot(a, b):
    return lax.dot_general(a, b, (((1,), (1,)), ((), ())), preferred_element_type=jnp.float32)


def tn_dot(a, b):
    return lax.dot_general(a, b, (((0,), (0,)), ((), ())), precision=exact, preferred_element_type=jnp.float32)


def hi_dot(a, b):
    return jnp.dot(a, b, precision=exact, preferred_element_type=jnp.float32)


def spread(fields):
    big = fields * SUB
    r = lax.broadcasted_iota(jnp.int32, (big, fields), 0) // SUB
    c = lax.broadcasted_iota(jnp.int32, (big, fields), 1)
    return (r == c).astype(jnp.float32)


def same_row(big):
    r = lax.broadcasted_iota(jnp.int32, (big, big), 0) % SUB
    c = lax.broadcasted_iota(jnp.int32, (big, big), 1) % SUB
    return r == c


def basis_kernel(r_ref, top_ref, bottom_ref, side_ref, dinv_ref, dn_ref, up_ref, rt_ref, lf_ref,
                 m_ref, x0_ref, x1_ref, x2_ref, acc_ref):
    fields, rows, cols = r_ref.shape
    slabs = rows // SUB
    last = slabs + 1
    big = fields * SUB
    wide = dinv_ref.shape[1]
    row = lax.broadcasted_iota(jnp.int32, (SUB, wide), 0)

    for k in range(fields):
        x0_ref[k, 0:SUB, :] = top_ref[k] * dinv_ref[0:SUB, :]
        x0_ref[k, rows + SUB:rows + 2 * SUB, :] = bottom_ref[k] * dinv_ref[rows + SUB:rows + 2 * SUB, :]

    @pl.loop(0, slabs)
    def _(i):
        scale = plane_rows(dinv_ref, (i + 1) * SUB)
        for k in range(fields):
            x0_ref[k, pl.ds(pl.multiple_of((i + 1) * SUB, SUB), SUB), 0:cols] = rows_of(r_ref, k, i * SUB) * scale[:, :cols]
            x0_ref[k, pl.ds(pl.multiple_of((i + 1) * SUB, SUB), SUB), cols:wide] = rows_of(side_ref, k, i * SUB) * scale[:, cols:]

    acc_ref[...] = jnp.zeros_like(acc_ref)

    def sweep(src, dst, i):
        at = pl.multiple_of(i * SUB, SUB)
        coefs = [plane_rows(ref, i * SUB) for ref in (dn_ref, up_ref, rt_ref, lf_ref)]
        olds, news = [], []
        for k in range(fields):
            here, new = stencil(src, k, i, last, coefs, row)
            if dst is not None:
                dst[k, pl.ds(at, SUB), :] = new
            olds.append(here[:, :cols])
            news.append(new[:, :cols])
        return olds, news

    for t, (src, dst) in enumerate(((x0_ref, x1_ref), (x1_ref, x2_ref), (x2_ref, None))):
        if dst is not None:
            sweep(src, dst, 0)
            sweep(src, dst, last)

        @pl.loop(1, last)
        def _(i, src=src, dst=dst, t=t):
            olds, news = sweep(src, dst, i)
            old_hi, old_lo = split(jnp.concatenate(olds, 0))
            new_hi, new_lo = split(jnp.concatenate(news, 0))
            acc_ref[t, 0] += nt_dot(old_hi, old_hi)
            acc_ref[t, 1] += nt_dot(old_hi, old_lo)
            acc_ref[t, 2] += nt_dot(old_hi, new_hi) + nt_dot(old_hi, new_lo) + nt_dot(old_lo, new_hi)

    gather = spread(fields)
    keep = same_row(big)
    for t in range(ITERS):
        cross = acc_ref[t, 1]
        even = hi_dot(jnp.where(keep, acc_ref[t, 0], 0.0), gather)
        m_ref[2 * t] = tn_dot(gather, even)
        crossed = tn_dot(gather, hi_dot(jnp.where(keep, cross, 0.0), gather))
        m_ref[2 * t] += crossed + crossed.T
        odd = hi_dot(jnp.where(keep, acc_ref[t, 2], 0.0), gather)
        m_ref[2 * t + 1] = tn_dot(gather, odd)


def small_solve(a, b):
    n = a.shape[0]
    row = lax.broadcasted_iota(jnp.int32, a.shape, 0)
    for p in range(n):
        inv = 1.0 / a[p:p + 1, p:p + 1]
        pa = a[p:p + 1, :] * inv
        pb = b[p:p + 1, :] * inv
        col = a[:, p:p + 1]
        a = jnp.where(row == p, pa, a - col * pa)
        b = jnp.where(row == p, pb, b - col * pb)
    return b


def coefficients(m, hankel_ref):
    n = m[0].shape[0]
    deg = ITERS + 1
    hankel_ref[...] = jnp.zeros_like(hankel_ref)
    for i in range(deg):
        for j in range(deg):
            if i + j < MOMENTS:
                hankel_ref[i * n:(i + 1) * n, j * n:(j + 1) * n] = m[i + j]
    hankel = hankel_ref[...]
    zero = jnp.zeros((n, n), jnp.float32)
    r = lax.broadcasted_iota(jnp.int32, (n, n), 0)
    c = lax.broadcasted_iota(jnp.int32, (n, n), 1)
    eye = (r == c).astype(jnp.float32)
    precond = jnp.concatenate([eye] + [zero] * (deg - 1), 0)
    direction = precond
    total = jnp.zeros_like(precond)
    gram_now = m[0]
    for it in range(ITERS):
        image = direction - jnp.concatenate([zero, direction[:-n]], 0)
        curvature = tn_dot(direction, hi_dot(hankel, image))
        alpha = small_solve(curvature, gram_now)
        total = total + hi_dot(direction, alpha)
        if it + 1 < ITERS:
            precond = precond - hi_dot(image, alpha)
            gram_next = tn_dot(precond, hi_dot(hankel, precond))
            beta = small_solve(gram_now, gram_next)
            direction = precond + hi_dot(direction, beta)
            gram_now = gram_next
    return total


def combine_kernel(m_ref, x0_ref, x1_ref, x2_ref, dinv_ref, dsq_ref, dn_ref, up_ref, rt_ref, lf_ref,
                   s_ref, res_ref, y_ref, hankel_ref, whi_ref, wlo_ref):
    fields, block, cols = s_ref.shape
    rows = x0_ref.shape[1] - 2 * SUB
    wide = x0_ref.shape[2]
    last = rows // SUB + 1
    big = fields * SUB
    g = pl.program_id(0)
    per = block // SUB
    row = lax.broadcasted_iota(jnp.int32, (SUB, wide), 0)

    @pl.when(g == 0)
    def _():
        total = coefficients([m_ref[j] for j in range(MOMENTS)], hankel_ref)
        out = spread(fields)
        keep = same_row(big)
        for j in range(ITERS):
            block_t = total[j * fields:(j + 1) * fields].T
            wide_t = lax.dot_general(hi_dot(out, block_t), out, (((1,), (1,)), ((), ())),
                                     precision=exact, preferred_element_type=jnp.float32)
            hi, lo = split(jnp.where(keep, wide_t, 0.0))
            whi_ref[:, j * big:(j + 1) * big] = hi
            wlo_ref[:, j * big:(j + 1) * big] = lo

    @pl.loop(jnp.where(g == 0, 0, g * per + 2), g * per + per + 2)
    def _(i):
        at = pl.multiple_of(i * SUB, SUB)
        stacked = jnp.concatenate([ref[k, pl.ds(at, SUB), :] for ref in (x0_ref, x1_ref, x2_ref) for k in range(fields)], 0)
        hi, lo = split(stacked)
        whi = whi_ref[...]
        y = (jnp.dot(whi, hi, preferred_element_type=jnp.float32)
             + jnp.dot(wlo_ref[...], hi, preferred_element_type=jnp.float32)
             + jnp.dot(whi, lo, preferred_element_type=jnp.float32))
        for k in range(fields):
            y_ref[k, pl.ds(at, SUB), :] = y[k * SUB:(k + 1) * SUB]

    @pl.loop(0, per)
    def _(q):
        i = g * per + q + 1
        at = pl.multiple_of(i * SUB, SUB)
        to = pl.multiple_of(q * SUB, SUB)
        coefs = [plane_rows(ref, i * SUB) for ref in (dn_ref, up_ref, rt_ref, lf_ref)]
        inv = plane_rows(dinv_ref, i * SUB)[:, :cols]
        root = plane_rows(dsq_ref, i * SUB)[:, :cols]
        for k in range(fields):
            here, swept = stencil(y_ref, k, i, last, coefs, row)
            here = here[:, :cols]
            s_ref[k, pl.ds(to, SUB), :] = here * inv
            res_ref[k, pl.ds(to, SUB), :] = root * (x0_ref[k, pl.ds(at, SUB), :][:, :cols] - here + swept[:, :cols])


def halo(cells, axis, dim):
    count = lax.axis_size(axis)
    size = cells.shape[dim]
    head = lax.slice_in_dim(cells, 0, DEPTH, axis=dim)
    tail = lax.slice_in_dim(cells, size - DEPTH, size, axis=dim)
    before = lax.ppermute(tail, axis, [(i, i + 1) for i in range(count - 1)])
    after = lax.ppermute(head, axis, [(i + 1, i) for i in range(count - 1)])
    return before, after


def shards(right_side, cond_x, cond_y, pad_mask):
    fields, rows, cols = right_side.shape
    wide = cols + LANE
    free = 1.0 - pad_mask.astype(jnp.float32)
    planes = jnp.stack([cond_x, cond_y, free])
    row_strip = jnp.concatenate([right_side[:, :DEPTH], right_side[:, rows - DEPTH:]], 1)
    row_strip = jnp.concatenate([row_strip, jnp.concatenate([planes[:, :DEPTH], planes[:, rows - DEPTH:]], 1)], 0)
    above, below = halo(row_strip, "row", 1)
    ends = [slice(0, DEPTH), slice(cols - DEPTH, cols)]

    def column_strip(e):
        mid = jnp.concatenate([right_side[:, :, e], planes[:, :, e]], 0)
        full = jnp.concatenate([above[:, :, e], mid, below[:, :, e]], 1)
        return jnp.swapaxes(full, 1, 2)

    strip = jnp.concatenate([column_strip(e) for e in ends], 1)
    left, right = halo(strip, "col", 1)
    gap = jnp.zeros((left.shape[0], LANE - 2 * DEPTH, left.shape[2]), jnp.float32)
    side = jnp.swapaxes(jnp.concatenate([right, gap, left], 1), 1, 2)
    edge = SUB - DEPTH
    top = jnp.pad(jnp.concatenate([above, side[:, :DEPTH]], 2), ((0, 0), (edge, 0), (0, 0)))
    bottom = jnp.pad(jnp.concatenate([below, side[:, DEPTH + rows:]], 2), ((0, 0), (0, edge), (0, 0)))
    side = side[:, DEPTH:DEPTH + rows]
    ext = jnp.concatenate([top[fields:], jnp.concatenate([planes, side[fields:]], 2), bottom[fields:]], 1)
    cx, cy, fr = ext[0], ext[1], ext[2]
    diagonal = fr * (cx + jnp.roll(cx, 1, 0) + cy + jnp.roll(cy, 1, 1)) + (1.0 - fr)
    root = jnp.sqrt(diagonal)
    dinv = 1.0 / root
    scale = fr * dinv
    to_down = cx * scale * jnp.roll(scale, -1, 0)
    to_up = jnp.roll(to_down, 1, 0)
    to_right = cy * scale * jnp.roll(scale, -1, 1)
    to_left = jnp.roll(to_right, 1, 1)

    ext_shape = (fields, rows + 2 * SUB, wide)
    big = fields * SUB
    field_out = FIELD(ext_shape)
    vmem = pl.BlockSpec(memory_space=pltpu.VMEM)
    m, x0, x1, x2 = pl.pallas_call(
        basis_kernel,
        out_shape=[jax.ShapeDtypeStruct((MOMENTS, fields, fields), jnp.float32)] + [field_out] * 3,
        in_specs=[vmem] * 9,
        out_specs=[vmem] * 4,
        scratch_shapes=[pltpu.VMEM((ITERS, 3, big, big), jnp.float32)],
        name="basis",
        compiler_params=pltpu.CompilerParams(vmem_limit_bytes=BASIS_LIMIT),
    )(right_side, top[:fields], bottom[:fields], side[:fields], dinv, to_down, to_up, to_right, to_left)
    m = lax.psum(m, ("row", "col"))
    block = 4 * SUB
    while rows % block:
        block //= 2
    whole = lambda shape: pl.BlockSpec(shape, lambda g: (0,) * len(shape))
    plane = whole((rows + 2 * SUB, wide))
    out_spec = pl.BlockSpec((fields, block, cols), lambda g: (0, g, 0))
    return tuple(pl.pallas_call(
        combine_kernel,
        grid=(rows // block,),
        out_shape=[jax.ShapeDtypeStruct(right_side.shape, jnp.float32)] * 2,
        in_specs=[vmem] * 10,
        out_specs=[out_spec] * 2,
        scratch_shapes=[
            pltpu.VMEM(ext_shape, jnp.float32),
            pltpu.VMEM(((ITERS + 1) * fields,) * 2, jnp.float32),
            pltpu.VMEM((big, ITERS * big), jnp.bfloat16),
            pltpu.VMEM((big, ITERS * big), jnp.bfloat16),
        ],
        name="combine",
        compiler_params=pltpu.CompilerParams(vmem_limit_bytes=COMBINE_LIMIT, dimension_semantics=("arbitrary",)),
    )(m, x0, x1, x2, dinv, root, to_down, to_up, to_right, to_left))


FIELD = lambda shape: jax.ShapeDtypeStruct(shape, jnp.float32)
BASIS_LIMIT = 60 * 2**20
COMBINE_LIMIT = 60 * 2**20


def solution(mesh):
    in_specs = (P(None, "row", "col"), P("row", "col"), P("row", "col"), P("row", "col"))
    out_specs = (P(None, "row", "col"), P(None, "row", "col"))
    return jax.shard_map(shards, mesh=mesh, in_specs=in_specs, out_specs=out_specs, check_vma=False)
```

time: 516 us -> 184 us (0.36); the launches traced: 509 us -> 183 us
  matrix products: 186 us -> 0 us
  Pallas kernels: 0 us -> 95.3 us
  other arithmetic: 101 us -> 10.9 us
  blocking collectives: 131 us -> 44.3 us
  local copies, waits for them, and re-layouts: 45.3 us -> 20.7 us
  starting transfers between devices: 30 us -> 11.3 us
  waiting for transfers between devices: 15 us -> 0.01 us
    dot_general x22 -> x0, matrix products: 184 us -> none  [the longest x8 95.2 us: gram(): return jnp.einsum('kab,lab->kl', left, right, precision=exact_precision)]
    pallas_call x0 -> x2, Pallas kernels: none -> 95.3 us  [the longest x1 56.3 us: shards(): pl.pallas_call(basis_kernel, out_shape=[jax.ShapeDtypeStruct((MOMENTS, fi...]
    psum x3 -> x1, blocking collectives: 131 us -> 44.3 us  [shards(): m = lax.psum(m, ('row', 'col'))]
    add x4 -> x0, other arithmetic: 63.9 us -> none  [the longest x3 61.2 us: shards(): pad_nodes * direction]
    another operation x25 -> x1, other arithmetic: 20.1 us -> 1.03 us  [shards(): planes = jnp.stack([cond_x, cond_y, free])]
    ppermute x14 -> x4, starting transfers between devices: 30 us -> 11.3 us  [the longest x2 8.61 us: halo(): before = lax.ppermute(tail, axis, [(i, i + 1) for i in range(count - 1)])]
    ppermute x14 -> x4, waiting for transfers between devices: 15 us -> 0.01 us  [the longest x2 0.01 us: halo(): before = lax.ppermute(tail, axis, [(i, i + 1) for i in range(count - 1)])]
    ppermute x6 -> x2, local copies, waits for them, and re-layouts: 15.3 us -> 4.91 us  [the longest x1 3.2 us: halo(): before = lax.ppermute(tail, axis, [(i, i + 1) for i in range(count - 1)])]
  transfers between devices with their start and end apart: 14 -> 4, of which waited for: 5 -> 0; matrix products, arithmetic and copies ran while one was open for 10% -> 7% of each run, Pallas kernels for 0% -> 0%
where the time goes in v1:
time: 184 us; the launch traced here: 183 us
  Pallas kernels  95.3 us (52%)
  blocking collectives  44.3 us (24%)
  local copies, waits for them, and re-layouts  20.7 us (11%)
  starting transfers between devices  11.3 us (6%)
  other arithmetic  10.9 us (6%)
    pallas_call x1, Pallas kernels, shards(): pl.pallas_call(basis_kernel, out_shape=[jax.ShapeDtypeStruct((MOMENTS, fi...  56.3 us
    psum x1, blocking collectives, shards(): m = lax.psum(m, ('row', 'col'))  44.3 us
    pallas_call x1, Pallas kernels, shards(): pl.pallas_call(combine_kernel, grid=(rows // block,), out_shape=[jax.Shap...  39 us
    ppermute x2, starting transfers between devices, halo(): before = lax.ppermute(tail, axis, [(i, i + 1) for i in range(count - 1)])  8.61 us
    slice x3, local copies, waits for them, and re-layouts, column_strip(): mid = jnp.concatenate([right_side[:, :, e], planes[:, :, e]], 0)  5.58 us
  transfers between devices with their start and end apart: 4, of which 0 were waited for; matrix products, arithmetic and copies ran while one was open for 7% of the time, Pallas kernels for 0%

profile of v1, /device:TPU:0, one launch (start us, length us, event | category | flops | bytes accessed | tf_op | source)
XLA Modules:
  0.0 183.4 jit_solution(11504218809193264596)
XLA Ops:
  0.6 1.1 fusion.8
  1.7 1.0 subtract_bitcast_fusion
  2.7 0.8 fusion.5
  3.5 0.7 fusion.10
  4.3 5.0 %collective-permute-start = (f32[19,4,384]{2,1,0:T(4,128)}, f32[19,4,384]{2,1,0:T(4,128)S(1)}, u32[]{:S(2)}, u32[]{:S(2)}) collective-permute-start(f32[19,4,384]{2,1,0:T(4,128)} %get-tuple-element.22), channel_id=1, source_target_pairs={{0,8},{8,16},{16,24},{1,9},{9,17},{17,25},{2,10},{10,18},{18,26},{... | collective-permute-start | bytes 350216 | tf_op jit(solution)/shard_map/ppermute | solution.py:231
  9.2 0.0 copy-start.3
  9.2 0.0 copy-start.4
  9.2 1.4 collective-permute-start.1
  10.7 4.3 %fusion.7 = (f32[16,256,4]{2,1,0:T(8,128)}, f32[16,256,4]{2,1,0:T(8,128)S(1)}) fusion(f32[16,256,384]{2,1,0:T(8,128)} %r_ref.1), kind=kLoop, calls=%fused_computation.35 | loop fusion | bytes 262144 | tf_op jit(solution)/shard_map/slice | solution.py:247
  15.0 0.9 pad_maximum_fusion.5
  15.8 1.1 copy.7
  17.0 0.2 copy.11
  17.1 2.2 %copy.16 = f32[16,256,4]{1,2,0:T(4,128)S(1)} copy(f32[16,256,4]{2,1,0:T(8,128)} %get-tuple-element.12) | data formatting | bytes 131072
  19.3 0.6 copy.17
  20.0 0.0 collective-permute-done
  20.0 0.1 fusion.11
  20.1 0.2 copy.8
  20.3 0.2 copy.12
  20.5 0.0 collective-permute-done.1
  20.5 0.9 fusion.12
  21.4 0.2 copy.9
  21.6 0.2 copy.13
  21.9 0.2 maximum_bitcast_fusion.1
  22.0 1.3 collective-permute-start.2
  23.3 0.8 maximum_bitcast_fusion.2
  24.1 3.7 %collective-permute-start.3 = (f32[19,4,264]{2,1,0:T(4,128)}, f32[19,4,264]{2,1,0:T(4,128)}, u32[]{:S(2)}, u32[]{:S(2)}) collective-permute-start(f32[19,4,264]{2,1,0:T(4,128)} %maximum_bitcast_fusion.2), channel_id=1, source_target_pairs={{0,1},{1,2},{2,3},{3,4},{4,5},{5,6},{6,7},{8,9},{9,10},{10,11},{11... | collective-permute-start | bytes 240776 | tf_op jit(solution)/shard_map/ppermute | solution.py:231
  27.8 0.1 pad.32.clone
  27.9 1.7 copy.14
  29.6 3.2 %copy.15 = f32[19,4,264]{1,2,0:T(8,128)} copy(f32[19,4,264]{2,1,0:T(4,128)} %collective-permute-done.3) | data formatting | bytes 160512 | tf_op jit(solution)/shard_map/ppermute | solution.py:231
  32.8 2.5 %maximum_bitcast_fusion = f32[19,264,128]{2,1,0:T(8,128)S(1)} fusion(f32[19,4,264]{1,2,0:T(8,128)} %copy.15, f32[19,4,264]{1,2,0:T(8,128)S(1)} %copy.14, f32[128]{0:T(128)S(1)} %pad.32.clone), kind=kLoop, calls=%fused_computation | loop fusion | flops 1284096 | bytes 2729216 | tf_op jit(solution)/shard_map/transpose | solution.py:254
  35.3 1.0 select_maximum_fusion
  36.3 0.7 slice.174.bottom_ref
  37.0 0.7 slice.172.top_ref
  37.8 0.0 copy-start.5
  37.8 1.5 slice.175.side_ref
  39.3 0.2 pad_maximum_fusion
  39.6 0.1 slice.183
  39.7 0.4 fusion.3
  40.2 0.2 slice.189
  40.4 0.1 slice.185
  40.5 0.9 broadcast_divide_fusion.dinv_ref
  41.4 0.4 maximum_multiply_fusion.1
  41.8 0.1 slice.191
  41.9 1.1 pad_maximum_fusion.2.lf_ref
  42.9 0.9 pad_maximum_fusion.1.up_ref
  43.8 56.3 %basis.1 = (f32[6,16,16]{2,1,0:T(8,128)}, f32[16,272,512]{2,1,0:T(8,128)}, f32[16,272,512]{2,1,0:T(8,128)}, f32[16,272,512]{2,1,0:T(8,128)}) custom-call(f32[16,256,384]{2,1,0:T(8,128)} %r_ref.1, f32[16,8,512]{2,1,0:T(8,128)} %slice.172.top_ref, f32[16,8,512]{2,1,0:T(8,128)} %slice.174.bottom_ref, f32[16,256,128]{2,1,0:T(8,128)} %slice.175.side_ref, ...), custom_call_target="tpu_custom_call" | custom-call | tf_op jit(solution)/shard_map/basis/pallas_call | solution.py:274
  100.1 44.3 %psum.7.m_ref = f32[6,16,16]{2,1,0:T(8,128)} all-reduce(f32[6,16,16]{2,1,0:T(8,128)} %get-tuple-element.6), channel_id=1, replica_groups=mesh['row'=4,'col'=8] {'row','col'}, use_global_device_ids=true, to_apply=%region_0.1 | all-reduce | flops 1536 | bytes 12288 | tf_op jit(solution)/shard_map/psum | solution.py:283
  144.4 39.0 %combine.1 = (f32[16,256,384]{2,1,0:T(8,128)}, f32[16,256,384]{2,1,0:T(8,128)}) custom-call(f32[6,16,16]{2,1,0:T(8,128)} %psum.7.m_ref, f32[16,272,512]{2,1,0:T(8,128)} %get-tuple-element.7.x0_ref, f32[16,272,512]{2,1,0:T(8,128)} %get-tuple-element.8.x1_ref, f32[16,272,512]{2,1,0:T(8,128)} %get-tuple-element.9.x2_ref, ...), custom_call_target="tpu_custom_call" | custom-call | tf_op jit(solution)/shard_map/combine/pallas_call | solution.py:290
  (21 shorter events, 0.2 us)
Async XLA Ops:
  4.3 15.7 %collective-permute-start = (f32[19,4,384]{2,1,0:T(4,128)}, f32[19,4,384]{2,1,0:T(4,128)S(1)}, u32[]{:S(2)}, u32[]{:S(2)}) collective-permute-start(f32[19,4,384]{2,1,0:T(4,128)} %get-tuple-element.22), channel_id=1, source_target_pairs={{0,8},{8,16},{16,24},{1,9},{9,17},{17,25},{2,10},{10,18},{18,26},{... | collective-permute-start | bytes 350216 | tf_op jit(solution)/shard_map/ppermute | solution.py:231
  9.2 5.7 %copy-start.3 = (f32[256,384]{1,0:T(8,128)S(1)}, f32[256,384]{1,0:T(8,128)}, u32[]{:S(2)}) copy-start(f32[256,384]{1,0:T(8,128)} %param.6) | copy-start | bytes 1179652
  9.2 5.7 %copy-start.4 = (f32[256,384]{1,0:T(8,128)S(1)}, f32[256,384]{1,0:T(8,128)}, u32[]{:S(2)}) copy-start(f32[256,384]{1,0:T(8,128)} %param.5) | copy-start | bytes 1179652
  9.2 11.3 %collective-permute-start.1 = (f32[19,4,384]{2,1,0:T(4,128)}, f32[19,4,384]{2,1,0:T(4,128)}, u32[]{:S(2)}, u32[]{:S(2)}) collective-permute-start(f32[19,4,384]{2,1,0:T(4,128)} %get-tuple-element.23), channel_id=1, source_target_pairs={{8,0},{16,8},{24,16},{9,1},{17,9},{25,17},{10,2},{18,10},{26,18},{... | collective-permute-start | bytes 350216 | tf_op jit(solution)/shard_map/ppermute | solution.py:232
  22.0 5.8 %collective-permute-start.2 = (f32[19,4,264]{2,1,0:T(4,128)S(1)}, f32[19,4,264]{2,1,0:T(4,128)}, u32[]{:S(2)}, u32[]{:S(2)}) collective-permute-start(f32[19,4,264]{2,1,0:T(4,128)S(1)} %maximum_bitcast_fusion.1), channel_id=1, source_target_pairs={{1,0},{2,1},{3,2},{4,3},{5,4},{6,5},{7,6},{9,8},{10,9},{11,10},{12... | collective-permute-start | bytes 240776 | tf_op jit(solution)/shard_map/ppermute | solution.py:232
  24.1 5.5 %collective-permute-start.3 = (f32[19,4,264]{2,1,0:T(4,128)}, f32[19,4,264]{2,1,0:T(4,128)}, u32[]{:S(2)}, u32[]{:S(2)}) collective-permute-start(f32[19,4,264]{2,1,0:T(4,128)} %maximum_bitcast_fusion.2), channel_id=1, source_target_pairs={{0,1},{1,2},{2,3},{3,4},{4,5},{5,6},{6,7},{8,9},{9,10},{10,11},{11... | collective-permute-start | bytes 240776 | tf_op jit(solution)/shard_map/ppermute | solution.py:231
  37.8 1.5 copy-start.5
  40.1 1.6 copy-start.2
  41.7 2.1 %copy-start = (f32[272,512]{1,0:T(8,128)}, f32[272,512]{1,0:T(8,128)S(1)}, u32[]{:S(2)}) copy-start(f32[272,512]{1,0:T(8,128)S(1)} %get-tuple-element.18.rt_ref) | copy-start | bytes 1671172
  41.7 2.1 %copy-start.1 = (f32[272,512]{1,0:T(8,128)}, f32[272,512]{1,0:T(8,128)S(1)}, u32[]{:S(2)}) copy-start(f32[272,512]{1,0:T(8,128)S(1)} %get-tuple-element.19.dn_ref) | copy-start | bytes 1671172

commit v2 on v1

--- a/solution.py
+++ b/solution.py
@@ -69,7 +69,7 @@
 
 
 def basis_kernel(r_ref, top_ref, bottom_ref, side_ref, dinv_ref, dn_ref, up_ref, rt_ref, lf_ref,
-                 m_ref, x0_ref, x1_ref, x2_ref, acc_ref):
+                 m_ref, x0_out, x1_out, x2_out, x0_ref, x1_ref, x2_ref, acc_ref, sems):
     fields, rows, cols = r_ref.shape
     slabs = rows // SUB
     last = slabs + 1
@@ -89,6 +89,8 @@
             x0_ref[k, pl.ds(pl.multiple_of((i + 1) * SUB, SUB), SUB), cols:wide] = rows_of(side_ref, k, i * SUB) * scale[:, cols:]
 
     acc_ref[...] = jnp.zeros_like(acc_ref)
+    copies = [pltpu.make_async_copy(a, b, sems.at[j]) for j, (a, b) in
+              enumerate(((x0_ref, x0_out), (x1_ref, x1_out), (x2_ref, x2_out)))]
 
     def sweep(src, dst, i):
         at = pl.multiple_of(i * SUB, SUB)
@@ -103,6 +105,7 @@
         return olds, news
 
     for t, (src, dst) in enumerate(((x0_ref, x1_ref), (x1_ref, x2_ref), (x2_ref, None))):
+        copies[t].start()
         if dst is not None:
             sweep(src, dst, 0)
             sweep(src, dst, last)
@@ -126,6 +129,8 @@
         m_ref[2 * t] += crossed + crossed.T
         odd = hi_dot(jnp.where(keep, acc_ref[t, 2], 0.0), gather)
         m_ref[2 * t + 1] = tn_dot(gather, odd)
+    for copy in copies:
+        copy.wait()
 
 
 def small_solve(a, b):
@@ -173,11 +178,10 @@
 
 
 def combine_kernel(m_ref, x0_ref, x1_ref, x2_ref, dinv_ref, dsq_ref, dn_ref, up_ref, rt_ref, lf_ref,
-                   s_ref, res_ref, y_ref, hankel_ref, whi_ref, wlo_ref):
+                   s_ref, res_ref, y_ref, diff_ref, hankel_ref, whi_ref, wlo_ref):
     fields, block, cols = s_ref.shape
-    rows = x0_ref.shape[1] - 2 * SUB
     wide = x0_ref.shape[2]
-    last = rows // SUB + 1
+    last = y_ref.shape[1] // SUB - 1
     big = fields * SUB
     g = pl.program_id(0)
     per = block // SUB
@@ -196,31 +200,35 @@
             whi_ref[:, j * big:(j + 1) * big] = hi
             wlo_ref[:, j * big:(j + 1) * big] = lo
 
-    @pl.loop(jnp.where(g == 0, 0, g * per + 2), g * per + per + 2)
-    def _(i):
-        at = pl.multiple_of(i * SUB, SUB)
-        stacked = jnp.concatenate([ref[k, pl.ds(at, SUB), :] for ref in (x0_ref, x1_ref, x2_ref) for k in range(fields)], 0)
+    @pl.loop(0, per)
+    def _(q):
+        frm = pl.multiple_of(q * SUB, SUB)
+        at = pl.multiple_of((g * per + q) * SUB, SUB)
+        stacked = jnp.concatenate([ref[k, pl.ds(frm, SUB), :] for ref in (x0_ref, x1_ref, x2_ref) for k in range(fields)], 0)
         hi, lo = split(stacked)
         whi = whi_ref[...]
         y = (jnp.dot(whi, hi, preferred_element_type=jnp.float32)
              + jnp.dot(wlo_ref[...], hi, preferred_element_type=jnp.float32)
              + jnp.dot(whi, lo, preferred_element_type=jnp.float32))
         for k in range(fields):
-            y_ref[k, pl.ds(at, SUB), :] = y[k * SUB:(k + 1) * SUB]
-
-    @pl.loop(0, per)
-    def _(q):
-        i = g * per + q + 1
-        at = pl.multiple_of(i * SUB, SUB)
-        to = pl.multiple_of(q * SUB, SUB)
-        coefs = [plane_rows(ref, i * SUB) for ref in (dn_ref, up_ref, rt_ref, lf_ref)]
-        inv = plane_rows(dinv_ref, i * SUB)[:, :cols]
-        root = plane_rows(dsq_ref, i * SUB)[:, :cols]
-        for k in range(fields):
-            here, swept = stencil(y_ref, k, i, last, coefs, row)
-            here = here[:, :cols]
-            s_ref[k, pl.ds(to, SUB), :] = here * inv
-            res_ref[k, pl.ds(to, SUB), :] = root * (x0_ref[k, pl.ds(at, SUB), :][:, :cols] - here + swept[:, :cols])
+            y_k = y[k * SUB:(k + 1) * SUB]
+            y_ref[k, pl.ds(at, SUB), :] = y_k
+            diff_ref[k, pl.ds(at, SUB), :] = stacked[k * SUB:(k + 1) * SUB, :cols] - y_k[:, :cols]
+
+    @pl.when(g > 0)
+    def _():
+        @pl.loop(0, per)
+        def _(q):
+            i = (g - 1) * per + q + 1
+            at = pl.multiple_of(i * SUB, SUB)
+            to = pl.multiple_of(q * SUB, SUB)
+            coefs = [plane_rows(ref, i * SUB) for ref in (dn_ref, up_ref, rt_ref, lf_ref)]
+            inv = plane_rows(dinv_ref, i * SUB)[:, :cols]
+            root = plane_rows(dsq_ref, i * SUB)[:, :cols]
+            for k in range(fields):
+                here, swept = stencil(y_ref, k, i, last, coefs, row)
+                s_ref[k, pl.ds(to, SUB), :] = here[:, :cols] * inv
+                res_ref[k, pl.ds(to, SUB), :] = root * (diff_ref[k, pl.ds(at, SUB), :] + swept[:, :cols])
 
 
 def halo(cells, axis, dim):
@@ -231,6 +239,23 @@
     before = lax.ppermute(tail, axis, [(i, i + 1) for i in range(count - 1)])
     after = lax.ppermute(head, axis, [(i + 1, i) for i in range(count - 1)])
     return before, after
+
+
+def summed(x, axes):
+    for axis in axes:
+        n = lax.axis_size(axis)
+        if n & (n - 1):
+            x = lax.psum(x, axis)
+            continue
+        step = 1
+        while step < n:
+            far = (n // step).bit_length() % 2 == 1
+            got = [lax.ppermute(x, axis, [(i, i ^ (step * o)) for i in range(n)]) for o in ((1, 2, 3) if far else (1,))]
+            x = x + got[0]
+            if far:
+                x = x + (got[1] + got[2])
+            step *= 4 if far else 2
+    return x
 
 
 def shards(right_side, cond_x, cond_y, pad_mask):
@@ -269,32 +294,31 @@
 
     ext_shape = (fields, rows + 2 * SUB, wide)
     big = fields * SUB
-    field_out = FIELD(ext_shape)
+    field_out = jax.ShapeDtypeStruct(ext_shape, jnp.float32)
     vmem = pl.BlockSpec(memory_space=pltpu.VMEM)
     m, x0, x1, x2 = pl.pallas_call(
         basis_kernel,
         out_shape=[jax.ShapeDtypeStruct((MOMENTS, fields, fields), jnp.float32)] + [field_out] * 3,
         in_specs=[vmem] * 9,
-        out_specs=[vmem] * 4,
-        scratch_shapes=[pltpu.VMEM((ITERS, 3, big, big), jnp.float32)],
+        out_specs=[vmem] + [pl.BlockSpec(memory_space=pl.ANY)] * 3,
+        scratch_shapes=[pltpu.VMEM(ext_shape, jnp.float32)] * 3 + [pltpu.VMEM((ITERS, 3, big, big), jnp.float32), pltpu.SemaphoreType.DMA((3,))],
         name="basis",
         compiler_params=pltpu.CompilerParams(vmem_limit_bytes=BASIS_LIMIT),
     )(right_side, top[:fields], bottom[:fields], side[:fields], dinv, to_down, to_up, to_right, to_left)
-    m = lax.psum(m, ("row", "col"))
-    block = 4 * SUB
-    while rows % block:
-        block //= 2
-    whole = lambda shape: pl.BlockSpec(shape, lambda g: (0,) * len(shape))
-    plane = whole((rows + 2 * SUB, wide))
-    out_spec = pl.BlockSpec((fields, block, cols), lambda g: (0, g, 0))
+    m = summed(m.reshape(-1, LANE), ("col", "row")).reshape(m.shape)
+    block = 2 * SUB
+    assert rows % block == 0 and cols % LANE == 0
+    x_spec = pl.BlockSpec((fields, block, wide), lambda g: (0, g, 0))
+    out_spec = pl.BlockSpec((fields, block, cols), lambda g: (0, jnp.maximum(g - 1, 0), 0))
     return tuple(pl.pallas_call(
         combine_kernel,
-        grid=(rows // block,),
+        grid=(rows // block + 1,),
         out_shape=[jax.ShapeDtypeStruct(right_side.shape, jnp.float32)] * 2,
-        in_specs=[vmem] * 10,
+        in_specs=[vmem] + [x_spec] * 3 + [vmem] * 6,
         out_specs=[out_spec] * 2,
         scratch_shapes=[
             pltpu.VMEM(ext_shape, jnp.float32),
+            pltpu.VMEM((fields, rows + 2 * SUB, cols), jnp.float32),
             pltpu.VMEM(((ITERS + 1) * fields,) * 2, jnp.float32),
             pltpu.VMEM((big, ITERS * big), jnp.bfloat16),
             pltpu.VMEM((big, ITERS * big), jnp.bfloat16),
@@ -304,7 +328,6 @@
     )(m, x0, x1, x2, dinv, root, to_down, to_up, to_right, to_left))
 
 
-FIELD = lambda shape: jax.ShapeDtypeStruct(shape, jnp.float32)
 BASIS_LIMIT = 60 * 2**20
 COMBINE_LIMIT = 60 * 2**20
 

time: 184 us -> 151 us (0.82)
  blocking collectives: 44.3 us -> 0 us
  starting transfers between devices: 11.3 us -> 23.7 us
  Pallas kernels: 95.3 us -> 85.3 us
  waiting for transfers between devices: 0.01 us -> 6.94 us
    psum x1 -> x0, blocking collectives: 44.3 us -> none  [shards(): m = lax.psum(m, ('row', 'col'))]
    ppermute x0 -> x7, starting transfers between devices: none -> 12.3 us  [summed(): lax.ppermute(x, axis, [(i, i ^ step * o) for i in range(n)])]
    ppermute x0 -> x7, waiting for transfers between devices: none -> 6.93 us  [summed(): lax.ppermute(x, axis, [(i, i ^ step * o) for i in range(n)])]
    pallas_call x1, Pallas kernels: 56.3 us -> 49.8 us  [shards(): pl.pallas_call(basis_kernel, out_shape=[jax.ShapeDtypeStruct((MOMENTS, fi...]
    pallas_call x1, Pallas kernels: 39 us -> 35.5 us  [shards(): pl.pallas_call(combine_kernel, grid=(rows // block + 1,), out_shape=[jax....]
  transfers between devices with their start and end apart: 4 -> 11, of which waited for: 0 -> 5; matrix products, arithmetic and copies ran while one was open for 7% -> 8% of each run, Pallas kernels for 0% -> 0%
where the time goes in v2:
time: 151 us; the launch traced here: 150 us
  Pallas kernels  85.3 us (56%)
  starting transfers between devices  23.7 us (16%)
  local copies, waits for them, and re-layouts  22.3 us (15%)
  other arithmetic  11 us (7%)
  waiting for transfers between devices  6.94 us (5%)
    pallas_call x1, Pallas kernels, shards(): pl.pallas_call(basis_kernel, out_shape=[jax.ShapeDtypeStruct((MOMENTS, fi...  49.8 us
    pallas_call x1, Pallas kernels, shards(): pl.pallas_call(combine_kernel, grid=(rows // block + 1,), out_shape=[jax....  35.5 us
    ppermute x7, starting transfers between devices, summed(): lax.ppermute(x, axis, [(i, i ^ step * o) for i in range(n)])  12.3 us
    ppermute x2, starting transfers between devices, halo(): before = lax.ppermute(tail, axis, [(i, i + 1) for i in range(count - 1)])  8.62 us
    ppermute x7, waiting for transfers between devices, summed(): lax.ppermute(x, axis, [(i, i ^ step * o) for i in range(n)])  6.93 us
    slice x3, local copies, waits for them, and re-layouts, column_strip(): mid = jnp.concatenate([right_side[:, :, e], planes[:, :, e]], 0)  5.58 us
    ppermute x1, local copies, waits for them, and re-layouts, halo(): before = lax.ppermute(tail, axis, [(i, i + 1) for i in range(count - 1)])  3.2 us
  transfers between devices with their start and end apart: 11, of which 5 were waited for; matrix products, arithmetic and copies ran while one was open for 8% of the time, Pallas kernels for 0%

profile of v2, /device:TPU:0, one launch (start us, length us, event | category | flops | bytes accessed | tf_op | source)
XLA Modules:
  0.0 150.0 jit_solution(5688810989221473534)
XLA Ops:
  0.6 1.1 fusion.8
  1.7 1.0 subtract_bitcast_fusion
  2.7 0.8 fusion.5
  3.5 0.7 fusion.10
  4.3 5.0 %collective-permute-start = (f32[19,4,384]{2,1,0:T(4,128)}, f32[19,4,384]{2,1,0:T(4,128)S(1)}, u32[]{:S(2)}, u32[]{:S(2)}) collective-permute-start(f32[19,4,384]{2,1,0:T(4,128)} %get-tuple-element.22), channel_id=1, source_target_pairs={{0,8},{8,16},{16,24},{1,9},{9,17},{17,25},{2,10},{10,18},{18,26},{... | collective-permute-start | bytes 350216 | tf_op jit(solution)/shard_map/ppermute | solution.py:239
  9.2 1.4 collective-permute-start.1
  10.7 4.3 %fusion.7 = (f32[16,256,4]{2,1,0:T(8,128)}, f32[16,256,4]{2,1,0:T(8,128)S(1)}) fusion(f32[16,256,384]{2,1,0:T(8,128)} %r_ref.1), kind=kLoop, calls=%fused_computation.37 | loop fusion | bytes 262144 | tf_op jit(solution)/shard_map/slice | solution.py:272
  15.0 0.9 pad_maximum_fusion.5
  15.8 1.1 copy.7
  17.1 2.2 %copy.16 = f32[16,256,4]{1,2,0:T(4,128)S(1)} copy(f32[16,256,4]{2,1,0:T(8,128)} %get-tuple-element.12) | data formatting | bytes 131072
  19.3 0.6 copy.17
  20.1 0.2 copy.8
  20.3 0.2 copy.12
  20.5 0.9 fusion.12
  21.4 0.2 copy.9
  21.6 0.2 copy.13
  22.0 1.3 collective-permute-start.2
  23.3 0.8 maximum_bitcast_fusion.2
  24.1 3.7 %collective-permute-start.3 = (f32[19,4,264]{2,1,0:T(4,128)}, f32[19,4,264]{2,1,0:T(4,128)}, u32[]{:S(2)}, u32[]{:S(2)}) collective-permute-start(f32[19,4,264]{2,1,0:T(4,128)} %maximum_bitcast_fusion.2), channel_id=1, source_target_pairs={{0,1},{1,2},{2,3},{3,4},{4,5},{5,6},{6,7},{8,9},{9,10},{10,11},{11... | collective-permute-start | bytes 240776 | tf_op jit(solution)/shard_map/ppermute | solution.py:239
  27.9 1.7 %copy.14 = f32[19,4,264]{1,2,0:T(8,128)S(1)} copy(f32[19,4,264]{2,1,0:T(4,128)} %collective-permute-done.2) | data formatting | bytes 160512 | tf_op jit(solution)/shard_map/ppermute | solution.py:240
  29.6 3.2 %copy.15 = f32[19,4,264]{1,2,0:T(8,128)} copy(f32[19,4,264]{2,1,0:T(4,128)} %collective-permute-done.3) | data formatting | bytes 160512 | tf_op jit(solution)/shard_map/ppermute | solution.py:239
  32.8 2.5 %maximum_bitcast_fusion = f32[19,264,128]{2,1,0:T(8,128)S(1)} fusion(f32[19,4,264]{1,2,0:T(8,128)} %copy.15, f32[19,4,264]{1,2,0:T(8,128)S(1)} %copy.14, f32[128]{0:T(128)S(1)} %pad.32.clone), kind=kLoop, calls=%fused_computation | loop fusion | flops 1284096 | bytes 2729216 | tf_op jit(solution)/shard_map/transpose | solution.py:279
  35.3 1.0 select_maximum_fusion
  36.3 0.7 slice.174.bottom_ref
  37.0 0.7 slice.172.top_ref
  37.8 1.5 %slice.175.side_ref = f32[16,256,128]{2,1,0:T(8,128)} slice(f32[19,264,128]{2,1,0:T(8,128)S(1)} %maximum_bitcast_fusion), slice={[0:16], [4:260], [0:128]} | slice | bytes 4194304 | tf_op jit(solution)/shard_map/slice | solution.py:307
  39.3 0.2 pad_maximum_fusion
  39.7 0.4 fusion.3
  40.2 0.2 slice.189
  40.5 0.9 broadcast_divide_fusion.dinv_ref
  41.4 0.3 maximum_multiply_fusion.1
  41.9 1.1 pad_maximum_fusion.2.lf_ref
  43.0 0.9 pad_maximum_fusion.1.up_ref
  43.8 49.8 %basis.1 = (f32[6,16,16]{2,1,0:T(8,128)}, f32[16,272,512]{2,1,0:T(8,128)}, f32[16,272,512]{2,1,0:T(8,128)}, f32[16,272,512]{2,1,0:T(8,128)}) custom-call(f32[16,256,384]{2,1,0:T(8,128)} %r_ref.1, f32[16,8,512]{2,1,0:T(8,128)} %slice.172.top_ref, f32[16,8,512]{2,1,0:T(8,128)} %slice.174.bottom_ref, f32[16,256,128]{2,1,0:T(8,128)} %slice.175.side_ref, ...), custom_call_target="tpu_custom_call" | custom-call | tf_op jit(solution)/shard_map/basis/pallas_call | solution.py:299
  93.7 0.9 reshape.12
  94.6 0.8 collective-permute-start.4
  95.4 0.8 collective-permute-done.4
  96.2 3.6 %collective-permute-start.7 = (f32[12,128]{1,0:T(8,128)S(1)}, f32[12,128]{1,0:T(8,128)S(1)}, u32[]{:S(2)}, u32[]{:S(2)}) collective-permute-start(f32[12,128]{1,0:T(8,128)S(1)} %add.43), channel_id=1, source_target_pairs={{0,6},{1,7},{2,4},{3,5},{4,2},{5,3},{6,0},{7,1},{8,14},{9,15},{10,... | collective-permute-start | bytes 18440 | tf_op jit(solution)/shard_map/ppermute | solution.py:253
  99.8 0.6 collective-permute-start.6
  100.4 1.5 collective-permute-start.5
  101.9 1.6 %collective-permute-done.6 = f32[12,128]{1,0:T(8,128)S(1)} collective-permute-done((f32[12,128]{1,0:T(8,128)S(1)}, f32[12,128]{1,0:T(8,128)S(1)}, u32[]{:S(2)}, u32[]{:S(2)}) %collective-permute-start.6) | collective-permute-done | bytes 6176 | tf_op jit(solution)/shard_map/ppermute | solution.py:253
  103.5 0.6 collective-permute-done.5
  104.1 5.3 %collective-permute-start.10 = (f32[12,128]{1,0:T(8,128)S(1)}, f32[12,128]{1,0:T(8,128)S(1)}, u32[]{:S(2)}, u32[]{:S(2)}) collective-permute-start(f32[12,128]{1,0:T(8,128)S(1)} %add_add_fusion.1), channel_id=1, source_target_pairs={{0,24},{8,16},{16,8},{24,0},{1,25},{9,17},{17,9},{25,1},{2,26},{10... | collective-permute-start | bytes 18440 | tf_op jit(solution)/shard_map/ppermute | solution.py:253
  109.3 0.6 collective-permute-start.8
  110.0 1.0 collective-permute-done.10
  110.9 2.9 %collective-permute-done.9 = f32[12,128]{1,0:T(8,128)S(1)} collective-permute-done((f32[12,128]{1,0:T(8,128)S(1)}, f32[12,128]{1,0:T(8,128)S(1)}, u32[]{:S(2)}, u32[]{:S(2)}) %collective-permute-start.9) | collective-permute-done | bytes 6176 | tf_op jit(solution)/shard_map/ppermute | solution.py:253
  113.9 0.7 reshape.13.m_ref
  114.6 35.5 %combine.1 = (f32[16,256,384]{2,1,0:T(8,128)}, f32[16,256,384]{2,1,0:T(8,128)}) custom-call(f32[6,16,16]{2,1,0:T(8,128)} %reshape.13.m_ref, f32[16,272,512]{2,1,0:T(8,128)} %get-tuple-element.7.x0_ref, f32[16,272,512]{2,1,0:T(8,128)} %get-tuple-element.8.x1_ref, f32[16,272,512]{2,1,0:T(8,128)} %get-tuple-element.9.x2_ref, ...), custom_call_target="tpu_custom_call" | custom-call | tf_op jit(solution)/shard_map/combine/pallas_call | solution.py:313
  (39 shorter events, 0.9 us)
Async XLA Ops:
  4.3 15.7 %collective-permute-start = (f32[19,4,384]{2,1,0:T(4,128)}, f32[19,4,384]{2,1,0:T(4,128)S(1)}, u32[]{:S(2)}, u32[]{:S(2)}) collective-permute-start(f32[19,4,384]{2,1,0:T(4,128)} %get-tuple-element.22), channel_id=1, source_target_pairs={{0,8},{8,16},{16,24},{1,9},{9,17},{17,25},{2,10},{10,18},{18,26},{... | collective-permute-start | bytes 350216 | tf_op jit(solution)/shard_map/ppermute | solution.py:239
  9.2 5.7 %copy-start.3 = (f32[256,384]{1,0:T(8,128)S(1)}, f32[256,384]{1,0:T(8,128)}, u32[]{:S(2)}) copy-start(f32[256,384]{1,0:T(8,128)} %param.6) | copy-start | bytes 1179652
  9.2 5.7 %copy-start.4 = (f32[256,384]{1,0:T(8,128)S(1)}, f32[256,384]{1,0:T(8,128)}, u32[]{:S(2)}) copy-start(f32[256,384]{1,0:T(8,128)} %param.5) | copy-start | bytes 1179652
  9.2 11.3 %collective-permute-start.1 = (f32[19,4,384]{2,1,0:T(4,128)}, f32[19,4,384]{2,1,0:T(4,128)}, u32[]{:S(2)}, u32[]{:S(2)}) collective-permute-start(f32[19,4,384]{2,1,0:T(4,128)} %get-tuple-element.23), channel_id=1, source_target_pairs={{8,0},{16,8},{24,16},{9,1},{17,9},{25,17},{10,2},{18,10},{26,18},{... | collective-permute-start | bytes 350216 | tf_op jit(solution)/shard_map/ppermute | solution.py:240
  22.0 5.8 %collective-permute-start.2 = (f32[19,4,264]{2,1,0:T(4,128)S(1)}, f32[19,4,264]{2,1,0:T(4,128)}, u32[]{:S(2)}, u32[]{:S(2)}) collective-permute-start(f32[19,4,264]{2,1,0:T(4,128)S(1)} %maximum_bitcast_fusion.1), channel_id=1, source_target_pairs={{1,0},{2,1},{3,2},{4,3},{5,4},{6,5},{7,6},{9,8},{10,9},{11,10},{12... | collective-permute-start | bytes 240776 | tf_op jit(solution)/shard_map/ppermute | solution.py:240
  24.1 5.5 %collective-permute-start.3 = (f32[19,4,264]{2,1,0:T(4,128)}, f32[19,4,264]{2,1,0:T(4,128)}, u32[]{:S(2)}, u32[]{:S(2)}) collective-permute-start(f32[19,4,264]{2,1,0:T(4,128)} %maximum_bitcast_fusion.2), channel_id=1, source_target_pairs={{0,1},{1,2},{2,3},{3,4},{4,5},{5,6},{6,7},{8,9},{9,10},{10,11},{11... | collective-permute-start | bytes 240776 | tf_op jit(solution)/shard_map/ppermute | solution.py:239
  37.8 1.5 %copy-start.5 = (f32[256,384]{1,0:T(8,128)S(1)}, f32[256,384]{1,0:T(8,128)}, u32[]{:S(2)}) copy-start(f32[256,384]{1,0:T(8,128)} %param.5) | copy-start | bytes 1179652
  40.1 1.6 %copy-start.2 = (f32[272,512]{1,0:T(8,128)}, f32[272,512]{1,0:T(8,128)S(1)}, u32[]{:S(2)}) copy-start(f32[272,512]{1,0:T(8,128)S(1)} %get-tuple-element.11.dsq_ref) | copy-start | bytes 1671172
  41.7 2.1 %copy-start = (f32[272,512]{1,0:T(8,128)}, f32[272,512]{1,0:T(8,128)S(1)}, u32[]{:S(2)}) copy-start(f32[272,512]{1,0:T(8,128)S(1)} %get-tuple-element.18.rt_ref) | copy-start | bytes 1671172
  41.8 2.1 %copy-start.1 = (f32[272,512]{1,0:T(8,128)}, f32[272,512]{1,0:T(8,128)S(1)}, u32[]{:S(2)}) copy-start(f32[272,512]{1,0:T(8,128)S(1)} %get-tuple-element.19.dn_ref) | copy-start | bytes 1671172
  94.6 1.7 %collective-permute-start.4 = (f32[12,128]{1,0:T(8,128)S(1)}, f32[12,128]{1,0:T(8,128)S(1)}, u32[]{:S(2)}, u32[]{:S(2)}) collective-permute-start(f32[12,128]{1,0:T(8,128)S(1)} %reshape.12), channel_id=1, source_target_pairs={{0,1},{1,0},{2,3},{3,2},{4,5},{5,4},{6,7},{7,6},{8,9},{9,8},{10,11... | collective-permute-start | bytes 18440 | tf_op jit(solution)/shard_map/ppermute | solution.py:253
  96.2 5.6 %collective-permute-start.7 = (f32[12,128]{1,0:T(8,128)S(1)}, f32[12,128]{1,0:T(8,128)S(1)}, u32[]{:S(2)}, u32[]{:S(2)}) collective-permute-start(f32[12,128]{1,0:T(8,128)S(1)} %add.43), channel_id=1, source_target_pairs={{0,6},{1,7},{2,4},{3,5},{4,2},{5,3},{6,0},{7,1},{8,14},{9,15},{10,... | collective-permute-start | bytes 18440 | tf_op jit(solution)/shard_map/ppermute | solution.py:253
  99.8 3.7 %collective-permute-start.6 = (f32[12,128]{1,0:T(8,128)S(1)}, f32[12,128]{1,0:T(8,128)S(1)}, u32[]{:S(2)}, u32[]{:S(2)}) collective-permute-start(f32[12,128]{1,0:T(8,128)S(1)} %add.43), channel_id=1, source_target_pairs={{0,4},{1,5},{2,6},{3,7},{4,0},{5,1},{6,2},{7,3},{8,12},{9,13},{10,... | collective-permute-start | bytes 18440 | tf_op jit(solution)/shard_map/ppermute | solution.py:253
  100.4 3.7 %collective-permute-start.5 = (f32[12,128]{1,0:T(8,128)S(1)}, f32[12,128]{1,0:T(8,128)S(1)}, u32[]{:S(2)}, u32[]{:S(2)}) collective-permute-start(f32[12,128]{1,0:T(8,128)S(1)} %add.43), channel_id=1, source_target_pairs={{0,2},{1,3},{2,0},{3,1},{4,6},{5,7},{6,4},{7,5},{8,10},{9,11},{10,... | collective-permute-start | bytes 18440 | tf_op jit(solution)/shard_map/ppermute | solution.py:253
  104.1 6.9 %collective-permute-start.10 = (f32[12,128]{1,0:T(8,128)S(1)}, f32[12,128]{1,0:T(8,128)S(1)}, u32[]{:S(2)}, u32[]{:S(2)}) collective-permute-start(f32[12,128]{1,0:T(8,128)S(1)} %add_add_fusion.1), channel_id=1, source_target_pairs={{0,24},{8,16},{16,8},{24,0},{1,25},{9,17},{17,9},{25,1},{2,26},{10... | collective-permute-start | bytes 18440 | tf_op jit(solution)/shard_map/ppermute | solution.py:253
  109.3 4.5 %collective-permute-start.9 = (f32[12,128]{1,0:T(8,128)S(1)}, f32[12,128]{1,0:T(8,128)S(1)}, u32[]{:S(2)}, u32[]{:S(2)}) collective-permute-start(f32[12,128]{1,0:T(8,128)S(1)} %add_add_fusion.1), channel_id=1, source_target_pairs={{0,16},{8,24},{16,0},{24,8},{1,17},{9,25},{17,1},{25,9},{2,18},{10... | collective-permute-start | bytes 18440 | tf_op jit(solution)/shard_map/ppermute | solution.py:253
  109.3 4.5 %collective-permute-start.8 = (f32[12,128]{1,0:T(8,128)S(1)}, f32[12,128]{1,0:T(8,128)S(1)}, u32[]{:S(2)}, u32[]{:S(2)}) collective-permute-start(f32[12,128]{1,0:T(8,128)S(1)} %add_add_fusion.1), channel_id=1, source_target_pairs={{0,8},{8,0},{16,24},{24,16},{1,9},{9,1},{17,25},{25,17},{2,10},{10... | collective-permute-start | bytes 18440 | tf_op jit(solution)/shard_map/ppermute | solution.py:253
